TPU v7x, 128 devices: a whole 4x4x4 slice. The times are simulated.
128 devices in a mesh: grp: 8 (over y, core), dom: 16 (over z, x).
Axes of the slice: x: 4, y: 4, z: 4, core: 2. Of those that a mesh axis runs over, the one named last changes fastest.
Arguments:
- diag_blocks: bfloat16 [2048, 384, 384], P(('grp', 'dom')), may hold values from -0.3125 to 0.3125
- face_in: bfloat16 [4096, 384, 384], P(('grp', 'dom')), may hold values from -0.3125 to 0.3125
- face_cross: bfloat16 [2048, 384, 384], P(('grp', 'dom')), may hold values from -0.3125 to 0.3125
- metric: float32 [2048, 384], P(('grp', 'dom')), may hold values from 0.5 to 2
- source_in: int32 [4096], P(('grp', 'dom')), may hold values from 0 to 15
- source_cross: int32 [2048], P(('grp', 'dom')), may hold values from 0 to 15
- orient_in: int32 [4096], P(('grp', 'dom')), may hold values from 0 to 7
- orient_cross: int32 [2048], P(('grp', 'dom')), may hold values from 0 to 7
- peer_in: int32 [4096, 1], P(('grp', 'dom')), may hold values from 0 to 15; in each aligned block of 32 rows (0 to 31, 32 to 63, ...) at most 3 rows name the same one
- peer_cross: int32 [2048, 1], P(('grp', 'dom')), may hold values from 0 to 7; in each aligned block of 16 rows (0 to 15, 16 to 31, ...) at most 3 rows name the same one
- target_in: int32 [4096], P(('grp', 'dom')), may hold values from 0 to 47
- target_cross: int32 [2048], P(('grp', 'dom')), may hold values from 0 to 47
Outputs:
- coarse_diag: float32 [2048, 2304], P('grp')
- coarse_face: float32 [2048, 6912], P('grp')
Inputs may be any that keep to these rules, and one draw needn't show every extreme that they name: `peer_in`: at most 3 records of one device name the same partition; on some device exactly 3 do. `peer_cross`: at most 3 records of one device name the same group; on some device exactly 3 do.
All inputs are finite; a program needn't handle non-finite values.
Results may differ from a plain program's by a relative error of at most 0.0052.
Values may be sent and summed in bfloat16 or wider, within the bound.
A program may use at most 128 MiB of HBM per device.

v0:
```python
import jax
import jax.numpy as jnp
from jax import lax
from jax.sharding import PartitionSpec as P


def corner_table(var_count):
    nodes = -1.0 + 2.0 * jnp.arange(4, dtype=jnp.float32) / 3.0
    basis = jnp.stack(((1.0 - nodes) / 2.0, (1.0 + nodes) / 2.0), axis=1)
    cube = jnp.einsum("ia,jb,kc->abcijk", basis, basis, basis).reshape(8, 64)
    return jnp.kron(jnp.eye(var_count, dtype=jnp.float32), cube)


def restrictor(weights, orient):
    var_count = weights.shape[1] // 64
    table = corner_table(var_count)
    full = weights[:, None, :] * table[None]
    shaped = full.reshape(weights.shape[0], var_count * 8, var_count, 4, 4, 4)
    bits = orient.reshape(-1, 1, 1, 1, 1, 1)
    shaped = jnp.where(bits % 2 == 1, jnp.flip(shaped, 3), shaped)
    shaped = jnp.where(bits // 2 % 2 == 1, jnp.flip(shaped, 4), shaped)
    shaped = jnp.where(bits // 4 % 2 == 1, jnp.flip(shaped, 5), shaped)
    return shaped.reshape(weights.shape[0], var_count * 8, var_count * 64).astype(jnp.bfloat16)


def pick_rows(index, table):
    picks = (index[:, None] == jnp.arange(table.shape[0], dtype=jnp.int32)[None, :]).astype(
        jnp.float32
    )
    return jnp.dot(picks, table, precision=lax.Precision.HIGHEST)


def place_rows(targets, values, row_count):
    picks = (jnp.arange(row_count, dtype=jnp.int32)[:, None] == targets[None, :]).astype(
        jnp.float32
    )
    return jnp.dot(picks, values, precision=lax.Precision.HIGHEST)


def one_sided(blocks, column_side):
    return jnp.einsum(
        "rcj,rij->rci", column_side, blocks, preferred_element_type=jnp.float32
    ).astype(jnp.bfloat16)


def coarse_terms(row_side, products):
    return jnp.einsum("rci,rdi->rcd", row_side, products, preferred_element_type=jnp.float32)


def pack_records(products, targets, peers, peer_count, capacity):
    count = products.shape[0]
    onehot = (peers[:, None] == jnp.arange(peer_count, dtype=jnp.int32)[None, :]).astype(jnp.int32)
    order_rank = jnp.sum((jnp.cumsum(onehot, axis=0) - 1) * onehot, axis=1)
    position = peers * capacity + order_rank
    places = jnp.arange(peer_count * capacity, dtype=jnp.int32)
    picks = places[:, None] == position[None, :]
    flattened = products.reshape(count, -1)
    packed = jnp.dot(
        picks.astype(jnp.bfloat16), flattened, preferred_element_type=jnp.float32
    ).astype(jnp.bfloat16)
    slot_ids = jnp.sum(jnp.where(picks, targets[None, :] + 1, 0), axis=1) - 1
    return (
        packed.reshape((peer_count, capacity) + products.shape[1:]),
        slot_ids.reshape(peer_count, capacity),
    )


def per_device(
    diag_blocks,
    face_in,
    face_cross,
    metric,
    source_in,
    source_cross,
    orient_in,
    orient_cross,
    peer_in,
    peer_cross,
    target_in,
    target_cross,
):
    elem_count = metric.shape[0]
    coarse_width = metric.shape[1] // 8
    square = coarse_width * coarse_width
    group_width = lax.axis_size("dom")
    group_count = lax.axis_size("grp")
    cross_capacity = (face_cross.shape[0] + group_count - 1) // group_count + 1
    inner_capacity = (face_in.shape[0] + group_width - 1) // group_width + 1

    def receive(packet):
        products, slot_ids = packet
        peers_here, items = slot_ids.shape
        flat_ids = slot_ids.reshape(-1)
        row_side = restrictor(
            pick_rows(flat_ids // 3, metric), jnp.zeros(flat_ids.shape, jnp.int32)
        )
        terms = coarse_terms(
            row_side, products.reshape(peers_here * items, products.shape[2], products.shape[3])
        )
        return (terms.reshape(peers_here, items, square), slot_ids)

    diag_side = restrictor(metric, jnp.zeros((elem_count,), jnp.int32))
    diag_coarse = coarse_terms(diag_side, one_sided(diag_blocks, diag_side)).reshape(
        elem_count, square
    )
    cross_side = restrictor(pick_rows(source_cross, metric), orient_cross)
    cross_products = one_sided(face_cross, cross_side)
    inner_side = restrictor(pick_rows(source_in, metric), orient_in)
    inner_products = one_sided(face_in, inner_side)
    cross_packed, cross_ids = pack_records(
        cross_products, target_cross, peer_cross[:, 0], group_count, cross_capacity
    )
    cross_terms, cross_got = receive(
        (
            lax.all_to_all(cross_packed, "grp", split_axis=0, concat_axis=0, tiled=True),
            lax.all_to_all(cross_ids, "grp", split_axis=0, concat_axis=0, tiled=True),
        )
    )
    inner_packed, inner_ids = pack_records(
        inner_products, target_in, peer_in[:, 0], group_width, inner_capacity
    )
    inner_terms, inner_got = receive(
        (
            lax.all_to_all(inner_packed, "dom", split_axis=0, concat_axis=0, tiled=True),
            lax.all_to_all(inner_ids, "dom", split_axis=0, concat_axis=0, tiled=True),
        )
    )
    face_local = place_rows(cross_got.reshape(-1), cross_terms.reshape(-1, square), 3 * elem_count)
    face_local = face_local + place_rows(
        inner_got.reshape(-1), inner_terms.reshape(-1, square), 3 * elem_count
    )
    face_local = face_local.reshape(elem_count, 3 * square)
    coarse_diag, coarse_face = (
        lax.all_gather(diag_coarse, "dom", axis=0, tiled=True),
        lax.all_gather(face_local, "dom", axis=0, tiled=True),
    )
    return (coarse_diag, coarse_face)


def solution(mesh):
    placed = (
        P(("grp", "dom"), None, None),
        P(("grp", "dom"), None, None),
        P(("grp", "dom"), None, None),
        P(("grp", "dom"), None),
        P(("grp", "dom")),
        P(("grp", "dom")),
        P(("grp", "dom")),
        P(("grp", "dom")),
        P(("grp", "dom"), None),
        P(("grp", "dom"), None),
        P(("grp", "dom")),
        P(("grp", "dom")),
    )
    return jax.shard_map(
        per_device,
        mesh=mesh,
        in_specs=placed,
        out_specs=(P("grp", None), P("grp", None)),
        check_vma=False,
    )
```

profile of v0, /device:TPU:1, one launch (start us, length us, event | category | flops | bytes accessed | tf_op | source)
XLA Modules:
  0.0 180.3 jit_solution(1263921991991287014)
XLA Ops:
  7.2 0.7 fusion.33
  7.9 0.8 select_reduce_fusion.3
  8.8 0.7 multiply_add_fusion.1
  9.4 0.1 select_reduce_fusion.2
  9.5 0.7 sub.80
  10.2 6.0 %all-to-all-start = ((s32[8,1,3]{2,1,0:T(1,128)}), s32[8,1,3]{2,1,0:T(1,128)S(1)}, u32[]{:S(2)}, u32[]{:S(2)}) async-start(s32[8,1,3]{2,1,0:T(1,128)} %bitcast.3), calls=%async_computation | async-start | bytes 8192 | tf_op jit(solution)/shard_map/all_to_all | solution.py:116
  16.2 0.1 broadcast_multiply_fusion.3
  16.3 0.1 multiply_bitcast_fusion
  16.4 0.1 mul.177
  16.5 0.1 copy.39
  16.6 0.1 mul.179
  16.7 0.1 mul.174
  16.8 0.1 mul.175
  16.9 0.1 copy.40
  17.0 4.3 %fusion.15 = f32[16,48,48]{2,1,0:T(8,128)S(1)} fusion(bf16[16,384,384]{2,1,0:T(8,128)(2,1)} %param.12, f32[48,384]{1,0:T(8,128)S(1)} %copy.40, f32[16,384]{1,0:T(8,128)} %param.15), kind=kOutput, calls=%fused_computation.25 | convolution fusion | flops 256278528 | bytes 4964352 | tf_op jit(solution)/shard_map/rci,rdi->rcd/dot_general | solution.py:47
  21.4 0.8 reshape.407
  22.3 0.4 fusion.34
  22.6 1.0 broadcast_multiply_fusion.1
  23.7 0.6 reverse_select_fusion.5
  24.3 0.7 reverse_select_fusion.4
  25.0 0.8 fusion.1
  25.8 0.1 slice-done.1
  25.9 1.8 fusion.12
  27.6 0.9 copy.51
  28.6 0.4 fusion.26
  29.0 1.9 %broadcast_multiply_fusion = bf16[32,48,6,4,4,4]{1,0,5,4,3,2:T(8,128)(2,1)S(1)} fusion(f32[48,6,4,4,4]{0,4,3,2,1:T(4,128)S(1)} %broadcast_multiply_fusion.2, f32[32,6,4,4,4]{0,4,3,2,1:T(4,128)S(1)} %bitcast.55), kind=kLoop, calls=%fused_computation.14 | loop fusion | flops 1179648 | bytes 1302528 | tf_op jit(solution)/shard_map/mul | solution.py:17
  31.0 0.1 fusion.25
  31.1 0.1 reduce_window_sum.23
  31.1 0.2 select_reduce_fusion.1
  31.3 1.0 reverse_select_fusion.2
  32.4 0.1 select_reduce_fusion
  32.5 1.5 reverse_select_fusion.1
  34.0 1.1 fusion
  35.1 0.7 sub.86
  35.8 7.6 %all-to-all-start.2 = ((s32[16,1,3]{2,1,0:T(1,128)}), s32[16,1,3]{2,1,0:T(1,128)S(1)}, u32[]{:S(2)}, u32[]{:S(2)}) async-start(s32[16,1,3]{2,1,0:T(1,128)} %bitcast.8), calls=%async_computation.2 | async-start | bytes 16384 | tf_op jit(solution)/shard_map/all_to_all | solution.py:125
  43.4 1.6 convolution_convert_fusion.1
  45.0 1.0 copy.52
  46.0 3.8 %all-to-all-done.2 = s32[16,1,3]{2,1,0:T(1,128)S(1)} async-done(((s32[16,1,3]{2,1,0:T(1,128)}), s32[16,1,3]{2,1,0:T(1,128)S(1)}, u32[]{:S(2)}, u32[]{:S(2)}) %all-to-all-start.2) | async-done | bytes 224 | tf_op jit(solution)/shard_map/all_to_all | solution.py:125
  49.9 6.1 %all-to-all-start.1 = ((bf16[8,3,48,384]{3,2,1,0:T(8,128)(2,1)}), bf16[8,3,48,384]{3,2,1,0:T(8,128)(2,1)}, u32[]{:S(2)}, u32[]{:S(2)}) async-start(bf16[8,3,48,384]{3,2,1,0:T(8,128)(2,1)} %bitcast.49), calls=%async_computation.1 | async-start | bytes 1769472 | tf_op jit(solution)/shard_map/all_to_all | solution.py:115
  55.9 7.7 %fusion.9 = bf16[32,48,384]{2,1,0:T(8,128)(2,1)S(1)} fusion(bf16[32,384,384]{2,1,0:T(8,128)(2,1)} %param.13, bf16[32,48,384]{1,0,2:T(8,128)(2,1)S(1)} %bitcast.42), kind=kOutput, calls=%fused_computation.22 | convolution fusion | flops 453574656 | bytes 11796480 | tf_op jit(solution)/shard_map/rcj,rij->rci/dot_general | solution.py:41
  63.7 0.3 copy.53
  63.9 0.7 convolution_convert_fusion
  64.7 1.4 copy.54
  66.1 3.1 %all-to-all-done.1 = bf16[8,3,48,384]{3,2,1,0:T(8,128)(2,1)} async-done(((bf16[8,3,48,384]{3,2,1,0:T(8,128)(2,1)}), bf16[8,3,48,384]{3,2,1,0:T(8,128)(2,1)}, u32[]{:S(2)}, u32[]{:S(2)}) %all-to-all-start.1) | async-done | bytes 884768 | tf_op jit(solution)/shard_map/all_to_all | solution.py:115
  69.3 3.7 %all-to-all-start.3 = ((bf16[16,3,48,384]{3,2,1,0:T(8,128)(2,1)}), bf16[16,3,48,384]{3,2,1,0:T(8,128)(2,1)S(1)}, u32[]{:S(2)}, u32[]{:S(2)}) async-start(bf16[16,3,48,384]{3,2,1,0:T(8,128)(2,1)} %bitcast.23), calls=%async_computation.3 | async-start | bytes 3538944 | tf_op jit(solution)/shard_map/all_to_all | solution.py:124
  73.0 0.0 all-gather.5.cloned.1.call-start
  73.0 0.5 broadcast.910
  73.5 0.7 reduce.6
  74.2 0.1 eq.232
  74.3 0.2 fusion.30
  74.5 0.7 reduce.7
  75.2 0.1 eq.251
  75.3 0.2 fusion.24
  75.5 1.6 fusion.16
  77.1 0.3 reshape_reshape.6
  77.4 0.3 fusion.23
  77.7 21.1 %all-to-all-done.3 = bf16[16,3,48,384]{3,2,1,0:T(8,128)(2,1)S(1)} async-done(((bf16[16,3,48,384]{3,2,1,0:T(8,128)(2,1)}), bf16[16,3,48,384]{3,2,1,0:T(8,128)(2,1)S(1)}, u32[]{:S(2)}, u32[]{:S(2)}) %all-to-all-start.3) | async-done | bytes 1769504 | tf_op jit(solution)/shard_map/all_to_all | solution.py:124
  98.9 0.7 fusion.4
  99.6 0.5 reshape_reshape.7
  100.2 0.3 convolution_add_fusion
  100.5 0.9 reshape.414
  101.4 62.3 %all-gather.5.cloned.1.call-done = f32[256,6912]{1,0:T(8,128)} async-done(((f32[16,6912]{1,0:T(8,128)}), f32[256,6912]{1,0:T(8,128)}) %all-gather.5.cloned.1.call-update) | async-done | bytes 7077904 | tf_op jit(solution)/shard_map/all_gather | solution.py:135
  163.8 3.2 %copy.65 = f32[256,2304]{1,0:T(8,128)} copy(f32[256,2304]{1,0:T(8,128)} %all-gather.3.cloned.1.call-done) | data formatting | bytes 4718592
  167.0 6.4 %copy.66 = f32[256,6912]{1,0:T(8,128)} copy(f32[256,6912]{1,0:T(8,128)} %all-gather.5.cloned.1.call-done) | data formatting | bytes 14155776
  (36 shorter events, 0.3 us)
Async XLA Ops:
  10.2 25.6 %all-to-all-start = ((s32[8,1,3]{2,1,0:T(1,128)}), s32[8,1,3]{2,1,0:T(1,128)S(1)}, u32[]{:S(2)}, u32[]{:S(2)}) async-start(s32[8,1,3]{2,1,0:T(1,128)} %bitcast.3), calls=%async_computation | async-start | bytes 8192 | tf_op jit(solution)/shard_map/all_to_all | solution.py:116
  16.2 85.3 %all-gather.3.cloned.1.call-start = ((), (), s32[]{:S(2)}) async-start(), calls=%async_computation.4 | async-start | bytes 2506752 | tf_op jit(solution)/shard_map/all_gather | solution.py:134
  17.0 5.2 %copy-start = (f32[16,384]{1,0:T(8,128)S(1)}, f32[16,384]{1,0:T(8,128)}, u32[]{:S(2)}) copy-start(f32[16,384]{1,0:T(8,128)} %param.15) | copy-start | bytes 73732
  17.0 5.2 %copy-start.2 = (s32[16]{0:T(128)S(1)}, s32[16]{0:T(128)}, u32[]{:S(2)}) copy-start(s32[16]{0:T(128)} %param.17) | copy-start | bytes 196
  17.0 8.7 %slice-start = ((s8[4718592]{0:T(1024)(128)(4,1)}), s8[524288]{0:T(1024)(128)(4,1)S(1)}, s32[]{:S(2)}) async-start(s8[4718592]{0:T(1024)(128)(4,1)} %bitcast.46), calls=%async_computation.6 | async-start | bytes 1048576
  21.4 2.3 %copy-start.5 = (s32[16]{0:T(128)S(1)}, s32[16]{0:T(128)}, u32[]{:S(2)}) copy-start(s32[16]{0:T(128)} %param.19) | copy-start | bytes 196
  23.7 2.2 %slice-start.1 = ((s8[4718592]{0:T(1024)(128)(4,1)}), s8[4194304]{0:T(1024)(128)(4,1)S(1)}, s32[]{:S(2)}) async-start(s8[4718592]{0:T(1024)(128)(4,1)} %bitcast.46), calls=%async_computation.7 | async-start | bytes 8388608
  25.9 2.7 %copy-start.3 = (s32[32]{0:T(128)S(1)}, s32[32]{0:T(128)}, u32[]{:S(2)}) copy-start(s32[32]{0:T(128)} %param.16) | copy-start | bytes 388
  29.0 2.0 %copy-start.6 = (s32[32]{0:T(128)S(1)}, s32[32]{0:T(128)}, u32[]{:S(2)}) copy-start(s32[32]{0:T(128)} %param.18) | copy-start | bytes 388
  29.0 2.0 %copy-start.1 = (s32[32,1]{0,1:T(1,128)S(1)}, s32[32,1]{0,1:T(1,128)}, u32[]{:S(2)}) copy-start(s32[32,1]{0,1:T(1,128)} %param.20) | copy-start | bytes 388
  31.3 1.1 copy-start.4
  35.8 14.0 %all-to-all-start.2 = ((s32[16,1,3]{2,1,0:T(1,128)}), s32[16,1,3]{2,1,0:T(1,128)S(1)}, u32[]{:S(2)}, u32[]{:S(2)}) async-start(s32[16,1,3]{2,1,0:T(1,128)} %bitcast.8), calls=%async_computation.2 | async-start | bytes 16384 | tf_op jit(solution)/shard_map/all_to_all | solution.py:125
  49.9 19.4 %all-to-all-start.1 = ((bf16[8,3,48,384]{3,2,1,0:T(8,128)(2,1)}), bf16[8,3,48,384]{3,2,1,0:T(8,128)(2,1)}, u32[]{:S(2)}, u32[]{:S(2)}) async-start(bf16[8,3,48,384]{3,2,1,0:T(8,128)(2,1)} %bitcast.49), calls=%async_computation.1 | async-start | bytes 1769472 | tf_op jit(solution)/shard_map/all_to_all | solution.py:115
  69.3 29.6 %all-to-all-start.3 = ((bf16[16,3,48,384]{3,2,1,0:T(8,128)(2,1)}), bf16[16,3,48,384]{3,2,1,0:T(8,128)(2,1)S(1)}, u32[]{:S(2)}, u32[]{:S(2)}) async-start(bf16[16,3,48,384]{3,2,1,0:T(8,128)(2,1)} %bitcast.23), calls=%async_computation.3 | async-start | bytes 3538944 | tf_op jit(solution)/shard_map/all_to_all | solution.py:124
  73.0 90.8 %all-gather.5.cloned.1.call-start = ((), (), s32[]{:S(2)}) async-start(), calls=%async_computation.5 | async-start | bytes 7520256 | tf_op jit(solution)/shard_map/all_gather | solution.py:135
Sparse Core Ops, SparseCore 0:
  22.4 46.2 all-gather.2
  101.5 62.1 all-gather.4
where the time goes:
time: 181 us; the launch traced here: 180 us
  waiting for transfers between devices  90.5 us (50%)
  starting transfers between devices  23.4 us (13%)
  matrix products  20.3 us (11%)
  local copies, waits for them, and re-layouts  18.6 us (10%)
  between operations  14.4 us (8%)
  other arithmetic  13.1 us (7%)
    all_gather x1, waiting for transfers between devices, per_device(): lax.all_gather(face_local, 'dom', axis=0, tiled=True)  62.3 us
    all_to_all x1, waiting for transfers between devices, per_device(): lax.all_to_all(inner_packed, 'dom', split_axis=0, concat_axis=0, tiled=True)  21.1 us
    unnamed x24, local copies, waits for them, and re-layouts  13.4 us
    dot_general x2, matrix products, one_sided(): jnp.einsum('rcj,rij->rci', column_side, blocks, preferred_element_type=jn...  9.53 us
    all_to_all x1, starting transfers between devices, per_device(): lax.all_to_all(inner_ids, 'dom', split_axis=0, concat_axis=0, tiled=True)  7.6 us
    dot_general x3, matrix products, coarse_terms(): jnp.einsum('rci,rdi->rcd', row_side, products, preferred_element_type=jnp...  6.65 us
    all_to_all x1, starting transfers between devices, per_device(): lax.all_to_all(cross_packed, 'grp', split_axis=0, concat_axis=0, tiled=True)  6.07 us
    all_to_all x1, starting transfers between devices, per_device(): lax.all_to_all(cross_ids, 'grp', split_axis=0, concat_axis=0, tiled=True)  5.96 us
  transfers between devices with their start and end apart: 6, of which 4 were waited for; matrix products, arithmetic and copies ran while one was open for 22% of the time, Pallas kernels for 0%

commit v1 on v0

--- a/solution.py
+++ b/solution.py
@@ -132,7 +132,9 @@
     face_local = face_local.reshape(elem_count, 3 * square)
     coarse_diag, coarse_face = (
         lax.all_gather(diag_coarse, "dom", axis=0, tiled=True),
-        lax.all_gather(face_local, "dom", axis=0, tiled=True),
+        jnp.concatenate(
+            lax.all_to_all(jnp.stack([face_local] * lax.axis_size("dom")), "dom", 0, 0), axis=0
+        ),
     )
     return (coarse_diag, coarse_face)
 

time: 181 us -> 238 us (1.31)
  waiting for transfers between devices: 90.5 us -> 137 us
  starting transfers between devices: 23.4 us -> 28.1 us
  local copies, waits for them, and re-layouts: 18.6 us -> 21.5 us
    all_gather x1, waiting for transfers between devices: 0.02 us -> 110 us  [per_device(): lax.all_gather(diag_coarse, 'dom', axis=0, tiled=True)]
    all_gather x1 -> x0, waiting for transfers between devices: 62.3 us -> none  [per_device(): lax.all_gather(face_local, 'dom', axis=0, tiled=True)]
    all_to_all x0 -> x1, starting transfers between devices: none -> 4.68 us  [per_device(): lax.all_to_all(jnp.stack([face_local] * lax.axis_size('dom')), 'dom', 0, 0)]
    another operation x0 -> x2, local copies, waits for them, and re-layouts: none -> 3.77 us  [per_device(): jnp.stack([face_local] * lax.axis_size('dom'))]
    unnamed x24 -> x20, local copies, waits for them, and re-layouts: 13.4 us -> 13.4 us
  transfers between devices with their start and end apart: 6 -> 6, of which waited for: 4 -> 4; matrix products, arithmetic and copies ran while one was open for 22% -> 16% of each run, Pallas kernels for 0% -> 0%
where the time goes in v1:
time: 238 us; the launch traced here: 237 us
  waiting for transfers between devices  137 us (58%)
  starting transfers between devices  28.1 us (12%)
  matrix products  22.5 us (9%)
  local copies, waits for them, and re-layouts  21.5 us (9%)
  between operations  14.4 us (6%)
  other arithmetic  13.7 us (6%)
    all_gather x1, waiting for transfers between devices, per_device(): lax.all_gather(diag_coarse, 'dom', axis=0, tiled=True)  110 us
    all_to_all x1, waiting for transfers between devices, per_device(): lax.all_to_all(inner_packed, 'dom', split_axis=0, concat_axis=0, tiled=True)  20.4 us
    unnamed x20, local copies, waits for them, and re-layouts  13.4 us
    dot_general x2, matrix products, one_sided(): jnp.einsum('rcj,rij->rci', column_side, blocks, preferred_element_type=jn...  9.53 us
    all_to_all x1, starting transfers between devices, per_device(): lax.all_to_all(inner_ids, 'dom', split_axis=0, concat_axis=0, tiled=True)  7.6 us
    dot_general x3, matrix products, coarse_terms(): jnp.einsum('rci,rdi->rcd', row_side, products, preferred_element_type=jnp...  7.44 us
    all_to_all x1, starting transfers between devices, per_device(): lax.all_to_all(cross_packed, 'grp', split_axis=0, concat_axis=0, tiled=True)  6.08 us
    all_to_all x1, starting transfers between devices, per_device(): lax.all_to_all(cross_ids, 'grp', split_axis=0, concat_axis=0, tiled=True)  5.96 us
  transfers between devices with their start and end apart: 6, of which 4 were waited for; matrix products, arithmetic and copies ran while one was open for 16% of the time, Pallas kernels for 0%

profile of v1, /device:TPU:1, one launch (start us, length us, event | category | flops | bytes accessed | tf_op | source)
XLA Modules:
  0.0 237.1 jit_solution(8077958131709520443)
XLA Ops:
  7.2 0.7 fusion.33
  7.9 0.8 select_reduce_fusion.3
  8.8 0.7 multiply_add_fusion.1
  9.4 0.1 select_reduce_fusion.2
  9.5 0.7 sub.80
  10.2 6.0 %all-to-all-start = ((s32[8,1,3]{2,1,0:T(1,128)}), s32[8,1,3]{2,1,0:T(1,128)S(1)}, u32[]{:S(2)}, u32[]{:S(2)}) async-start(s32[8,1,3]{2,1,0:T(1,128)} %bitcast.3), calls=%async_computation | async-start | bytes 8192 | tf_op jit(solution)/shard_map/all_to_all | solution.py:116
  16.2 0.1 broadcast_multiply_fusion.3
  16.3 0.1 multiply_bitcast_fusion
  16.4 0.1 mul.177
  16.5 0.1 copy.39
  16.6 0.1 mul.179
  16.7 0.1 mul.174
  16.8 0.1 mul.175
  16.9 0.7 fusion.39
  17.6 1.1 fusion.34
  18.7 1.0 broadcast_multiply_fusion.1
  19.7 0.6 reverse_select_fusion.5
  20.3 0.7 reverse_select_fusion.4
  21.0 0.8 fusion.1
  21.8 0.1 slice-done.1
  21.9 1.8 fusion.12
  23.7 0.9 copy.51
  24.6 0.4 fusion.26
  25.0 1.9 broadcast_multiply_fusion
  27.2 0.2 select_reduce_fusion.1
  27.4 0.1 select_reduce_fusion
  27.5 1.0 reverse_select_fusion.2
  28.5 1.5 reverse_select_fusion.1
  30.0 1.1 fusion
  31.2 0.7 sub.86
  31.9 7.6 %all-to-all-start.2 = ((s32[16,1,3]{2,1,0:T(1,128)}), s32[16,1,3]{2,1,0:T(1,128)S(1)}, u32[]{:S(2)}, u32[]{:S(2)}) async-start(s32[16,1,3]{2,1,0:T(1,128)} %bitcast.8), calls=%async_computation.2 | async-start | bytes 16384 | tf_op jit(solution)/shard_map/all_to_all | solution.py:125
  39.5 1.6 convolution_convert_fusion.1
  41.0 1.0 copy.52
  42.0 3.8 %all-to-all-done.2 = s32[16,1,3]{2,1,0:T(1,128)S(1)} async-done(((s32[16,1,3]{2,1,0:T(1,128)}), s32[16,1,3]{2,1,0:T(1,128)S(1)}, u32[]{:S(2)}, u32[]{:S(2)}) %all-to-all-start.2) | async-done | bytes 224 | tf_op jit(solution)/shard_map/all_to_all | solution.py:125
  45.9 6.1 %all-to-all-start.1 = ((bf16[8,3,48,384]{3,2,1,0:T(8,128)(2,1)}), bf16[8,3,48,384]{3,2,1,0:T(8,128)(2,1)}, u32[]{:S(2)}, u32[]{:S(2)}) async-start(bf16[8,3,48,384]{3,2,1,0:T(8,128)(2,1)} %bitcast.50), calls=%async_computation.1 | async-start | bytes 1769472 | tf_op jit(solution)/shard_map/all_to_all | solution.py:115
  52.0 7.7 %fusion.9 = bf16[32,48,384]{2,1,0:T(8,128)(2,1)S(1)} fusion(bf16[32,384,384]{2,1,0:T(8,128)(2,1)} %param.13, bf16[32,48,384]{1,0,2:T(8,128)(2,1)S(1)} %bitcast.43), kind=kOutput, calls=%fused_computation.22 | convolution fusion | flops 453574656 | bytes 11796480 | tf_op jit(solution)/shard_map/rcj,rij->rci/dot_general | solution.py:41
  59.7 0.3 copy.53
  60.0 0.7 convolution_convert_fusion
  60.7 1.4 copy.54
  62.1 3.1 %all-to-all-done.1 = bf16[8,3,48,384]{3,2,1,0:T(8,128)(2,1)} async-done(((bf16[8,3,48,384]{3,2,1,0:T(8,128)(2,1)}), bf16[8,3,48,384]{3,2,1,0:T(8,128)(2,1)}, u32[]{:S(2)}, u32[]{:S(2)}) %all-to-all-start.1) | async-done | bytes 884768 | tf_op jit(solution)/shard_map/all_to_all | solution.py:115
  65.3 3.7 %all-to-all-start.3 = ((bf16[16,3,48,384]{3,2,1,0:T(8,128)(2,1)}), bf16[16,3,48,384]{3,2,1,0:T(8,128)(2,1)S(1)}, u32[]{:S(2)}, u32[]{:S(2)}) async-start(bf16[16,3,48,384]{3,2,1,0:T(8,128)(2,1)} %bitcast.24), calls=%async_computation.3 | async-start | bytes 3538944 | tf_op jit(solution)/shard_map/all_to_all | solution.py:124
  69.0 0.1 copy.40
  69.1 0.5 broadcast.911
  69.6 0.7 reduce.6
  70.3 0.1 eq.232
  70.4 0.2 fusion.30
  70.6 0.7 reduce.7
  71.3 0.1 eq.251
  71.4 0.9 fusion.24
  72.3 1.6 fusion.16
  73.9 0.3 reshape_reshape.6
  74.1 0.3 fusion.23
  74.5 20.4 %all-to-all-done.3 = bf16[16,3,48,384]{3,2,1,0:T(8,128)(2,1)S(1)} async-done(((bf16[16,3,48,384]{3,2,1,0:T(8,128)(2,1)}), bf16[16,3,48,384]{3,2,1,0:T(8,128)(2,1)S(1)}, u32[]{:S(2)}, u32[]{:S(2)}) %all-to-all-start.3) | async-done | bytes 1769504 | tf_op jit(solution)/shard_map/all_to_all | solution.py:124
  94.9 1.6 fusion.4
  96.5 0.5 reshape_reshape.7
  97.1 0.3 convolution_add_fusion
  97.4 0.1 stack_reshape.2
  97.6 3.6 %stack.5 = f32[16,16,6912]{2,1,0:T(8,128)} broadcast(f32[16,6912]{1,0:T(8,128)S(1)} %stack_reshape.2), dimensions={1,2} | broadcast | bytes 7520256 | tf_op jit(solution)/shard_map/stack | solution.py:136
  101.2 4.7 %all-to-all-start.4 = ((f32[16,16,6912]{2,1,0:T(8,128)}), f32[16,16,6912]{2,1,0:T(8,128)}, u32[]{:S(2)}, u32[]{:S(2)}) async-start(f32[16,16,6912]{2,1,0:T(8,128)} %stack.5), calls=%async_computation.4 | async-start | bytes 14155776 | tf_op jit(solution)/shard_map/all_to_all | solution.py:136
  105.9 4.2 %fusion.15 = f32[16,48,48]{2,1,0:T(8,128)S(1)} fusion(bf16[16,384,384]{2,1,0:T(8,128)(2,1)} %param.12, f32[48,384]{1,0:T(8,128)S(1)} %copy.40, f32[16,384]{1,0:T(8,128)S(1)} %copy-done), kind=kOutput, calls=%fused_computation.25 | convolution fusion | flops 256278528 | bytes 4964352 | tf_op jit(solution)/shard_map/rci,rdi->rcd/dot_general | solution.py:47
  110.2 0.9 reshape.409
  111.1 109.6 %all-gather.2.cloned.1.call-done = f32[256,2304]{1,0:T(8,128)} async-done(((f32[16,2304]{1,0:T(8,128)}), f32[256,2304]{1,0:T(8,128)}) %all-gather.2.cloned.1.call-update) | async-done | bytes 2359312 | tf_op jit(solution)/shard_map/all_gather | solution.py:134
  220.7 3.2 %copy.65 = f32[256,2304]{1,0:T(8,128)} copy(f32[256,2304]{1,0:T(8,128)} %all-gather.2.cloned.1.call-done) | data formatting | bytes 4718592
  223.9 6.4 %copy.66 = f32[256,6912]{1,0:T(8,128)} copy(f32[256,6912]{1,0:T(8,128)} %bitcast.12) | data formatting | bytes 14155776
  (32 shorter events, 0.4 us)
Async XLA Ops:
  10.2 21.6 %all-to-all-start = ((s32[8,1,3]{2,1,0:T(1,128)}), s32[8,1,3]{2,1,0:T(1,128)S(1)}, u32[]{:S(2)}, u32[]{:S(2)}) async-start(s32[8,1,3]{2,1,0:T(1,128)} %bitcast.3), calls=%async_computation | async-start | bytes 8192 | tf_op jit(solution)/shard_map/all_to_all | solution.py:116
  16.3 5.5 %slice-start = ((s8[4718592]{0:T(1024)(128)(4,1)}), s8[524288]{0:T(1024)(128)(4,1)S(1)}, s32[]{:S(2)}) async-start(s8[4718592]{0:T(1024)(128)(4,1)} %bitcast.47), calls=%async_computation.6 | async-start | bytes 1048576
  19.7 2.2 slice-start.1
  21.9 2.7 %copy-start = (f32[16,384]{1,0:T(8,128)S(1)}, f32[16,384]{1,0:T(8,128)}, u32[]{:S(2)}) copy-start(f32[16,384]{1,0:T(8,128)} %param.15) | copy-start | bytes 73732
  21.9 2.7 %copy-start.2 = (s32[32]{0:T(128)S(1)}, s32[32]{0:T(128)}, u32[]{:S(2)}) copy-start(s32[32]{0:T(128)} %param.16) | copy-start | bytes 388
  25.0 2.0 copy-start.4
  25.0 2.0 copy-start.1
  25.0 2.3 copy-start.3
  31.9 14.0 %all-to-all-start.2 = ((s32[16,1,3]{2,1,0:T(1,128)}), s32[16,1,3]{2,1,0:T(1,128)S(1)}, u32[]{:S(2)}, u32[]{:S(2)}) async-start(s32[16,1,3]{2,1,0:T(1,128)} %bitcast.8), calls=%async_computation.2 | async-start | bytes 16384 | tf_op jit(solution)/shard_map/all_to_all | solution.py:125
  45.9 19.4 %all-to-all-start.1 = ((bf16[8,3,48,384]{3,2,1,0:T(8,128)(2,1)}), bf16[8,3,48,384]{3,2,1,0:T(8,128)(2,1)}, u32[]{:S(2)}, u32[]{:S(2)}) async-start(bf16[8,3,48,384]{3,2,1,0:T(8,128)(2,1)} %bitcast.50), calls=%async_computation.1 | async-start | bytes 1769472 | tf_op jit(solution)/shard_map/all_to_all | solution.py:115
  65.3 29.6 %all-to-all-start.3 = ((bf16[16,3,48,384]{3,2,1,0:T(8,128)(2,1)}), bf16[16,3,48,384]{3,2,1,0:T(8,128)(2,1)S(1)}, u32[]{:S(2)}, u32[]{:S(2)}) async-start(bf16[16,3,48,384]{3,2,1,0:T(8,128)(2,1)} %bitcast.24), calls=%async_computation.3 | async-start | bytes 3538944 | tf_op jit(solution)/shard_map/all_to_all | solution.py:124
  101.2 119.4 %all-to-all-start.4 = ((f32[16,16,6912]{2,1,0:T(8,128)}), f32[16,16,6912]{2,1,0:T(8,128)}, u32[]{:S(2)}, u32[]{:S(2)}) async-start(f32[16,16,6912]{2,1,0:T(8,128)} %stack.5), calls=%async_computation.4 | async-start | bytes 14155776 | tf_op jit(solution)/shard_map/all_to_all | solution.py:136
  105.9 114.8 %all-gather.2.cloned.1.call-start = ((), (), s32[]{:S(2)}) async-start(), calls=%async_computation.5 | async-start | bytes 2506752 | tf_op jit(solution)/shard_map/all_gather | solution.py:134
Sparse Core Ops, SparseCore 0:
  111.2 109.4 all-gather.1
